TPU v7x, 512 devices: a whole 4x8x8 slice. The times are simulated.
512 devices in a mesh: pool: 32 (over z, x), tp: 16 (over y, core).
Axes of the slice: x: 4, y: 8, z: 8, core: 2. Of those that a mesh axis runs over, the one named last changes fastest.
Arguments:
- activations: bfloat16 [2, 256, 8192], P(None, None, 'tp'), may hold values from -6 to 6
- gate_matrix: bfloat16 [8192, 28672], P('tp', 'pool'), may hold values from -0.0625 to 0.0625
- up_weight: bfloat16 [8192, 28672], P('tp', 'pool'), may hold values from -0.0625 to 0.0625
- down_matrix: bfloat16 [28672, 8192], P('pool', 'tp'), may hold values from -0.03125 to 0.03125
- shrink_pages: bfloat16 [128, 64, 8192], P('pool', None, 'tp'), may hold values from -0.0625 to 0.0625
- expand_pages: bfloat16 [128, 64, 28672], P('pool', 'tp'), may hold values from -0.75 to 0.75
- row_adapter: int32 [2, 256], replicated, may hold values from 0 to 127, as said below
- page_table: int32 [128], replicated, may hold values from 0 to 127, as said below
Outputs:
- layer_out: bfloat16 [2, 256, 8192], P(None, None, 'tp')
Inputs may be any that keep to these rules, and one draw needn't show every extreme that they name: `row_adapter`: in each micro-batch, the rows use at most 1 distinct adapter among those whose pages have the same owner, the owner of page g being g // 4 (so a micro-batch may use up to 32 adapters, one per owner). A permutation: adapter a is stored at page page_table[a].
All inputs are finite; a program needn't handle non-finite values.
Results may differ from a plain program's by a relative error of at most 0.0057.
Values may be sent and summed in bfloat16 or wider, within the bound.
A program may use at most 64 MiB of HBM per device.

v0:
```python
import functools
import jax
import jax.numpy as jnp
from jax import lax
from jax.sharding import Mesh
from jax.sharding import PartitionSpec as P

CAP = 1
POOL = ("pool_0", "pool_1")
adapter_scale = 2.0


def in_blocks(value, dim, size):
    before, after = (value.shape[:dim], value.shape[dim + 1 :])
    return jnp.moveaxis(value.reshape(*before, size, -1, *after), dim, 0)


def sum_at_owner(value, axis, dim):
    size = lax.axis_size(axis)
    pieces = lax.all_to_all(in_blocks(value, dim, size), axis, 0, 0, tiled=True)
    return jnp.sum(pieces, axis=0)


def copy_for_each(value, axis):
    copies = jnp.broadcast_to(value, (lax.axis_size(axis), *value.shape))
    return lax.all_to_all(copies, axis, split_axis=0, concat_axis=0, tiled=True)


def over_copies(value, axis):
    everything = copy_for_each(value, axis)
    return jnp.sum(everything, axis=0)


def by_axis(value, axes):
    return functools.reduce(lax.psum, axes, value)


def on_device(
    activations,
    gate_matrix,
    up_weight,
    down_matrix,
    shrink_pages,
    expand_pages,
    row_adapter,
    page_table,
):
    pool_count = lax.axis_size(POOL)
    pool_index = lax.axis_index(POOL)
    batches, row_count, local_width = activations.shape
    page_count = shrink_pages.shape[0]
    rank_local = expand_pages.shape[1]
    hidden_local = gate_matrix.shape[1]
    adapter_total = page_table.shape[0]
    catalog = jnp.arange(adapter_total, dtype=jnp.int32)
    page_of_row = jnp.sum(jnp.where(row_adapter[:, :, None] == catalog, page_table, 0), axis=2)
    groups = [(batch_index, batch_index + 1) for batch_index in range(batches)]
    outputs = []
    for group_start, group_stop in groups:
        group_size = group_stop - group_start
        rows_in = activations[group_start:group_stop].reshape(group_size * row_count, local_width)
        pages_in = page_of_row[group_start:group_stop]
        row_pages = pages_in.reshape(-1)
        row_owner = row_pages // page_count
        row_local = row_pages % page_count
        row_total = group_size * row_count
        projected = jnp.einsum(
            "nd,prd->npr", rows_in, shrink_pages, preferred_element_type=jnp.float32
        )
        owned_here = (row_owner == pool_index)[:, None] & (
            row_local[:, None] == jnp.arange(page_count, dtype=jnp.int32)
        )
        shrink_part = jnp.sum(jnp.where(owned_here[:, :, None], projected, 0.0), axis=1)
        rank_share = sum_at_owner(shrink_part, "tp", 1)
        shrink_mine = over_copies(rank_share, POOL).astype(jnp.bfloat16)
        page_used = jnp.any(pages_in[:, :, None] == catalog, axis=1)
        page_order = jnp.cumsum(page_used.astype(jnp.int32), axis=1) - 1
        owner_order = (
            page_order.reshape(group_size, pool_count, page_count)
            - lax.dynamic_index_in_dim(page_order.reshape(group_size, pool_count, page_count), 0, 2)
            + page_used.reshape(group_size, pool_count, page_count)[:, :, :1].astype(jnp.int32)
            - 1
        )
        owned_used = lax.dynamic_index_in_dim(
            page_used.reshape(group_size, pool_count, page_count), pool_index, 1, keepdims=False
        )
        owned_order = lax.dynamic_index_in_dim(owner_order, pool_index, 1, keepdims=False)
        hit_table = owned_used[:, :, None] & (
            owned_order[:, :, None] == jnp.arange(CAP, dtype=jnp.int32)
        )
        chosen = jnp.sum(
            jnp.where(hit_table, jnp.arange(page_count, dtype=jnp.int32)[None, :, None], 0), axis=1
        )
        outgoing = jnp.take(expand_pages, chosen.reshape(-1), axis=0)
        outgoing = outgoing.reshape(group_size * CAP, rank_local, pool_count, hidden_local)
        received = lax.all_to_all(outgoing, POOL, split_axis=2, concat_axis=0, tiled=True)
        blocks_mat = received.reshape(pool_count * group_size * CAP * rank_local, hidden_local)
        slot_total = pool_count * group_size * CAP
        flat_order = owner_order.reshape(group_size, adapter_total)
        row_order = jnp.sum(
            jnp.where(pages_in[:, :, None] == catalog, flat_order[:, None, :], 0), axis=2
        )
        batch_of_row = lax.broadcasted_iota(jnp.int32, (group_size, row_count), 0)
        slot_of_row = (
            (pages_in // page_count * group_size + batch_of_row) * CAP + row_order
        ).reshape(-1)
        onehot = slot_of_row[:, None] == jnp.arange(slot_total, dtype=jnp.int32)
        wide_rows = jnp.where(
            onehot[:, :, None], shrink_mine[:, None, :], jnp.zeros((), jnp.bfloat16)
        )
        wide_rows = wide_rows.reshape(row_total, slot_total * rank_local)
        gate_term = jnp.dot(rows_in, gate_matrix, preferred_element_type=jnp.float32)
        up_product = jnp.dot(rows_in, up_weight, preferred_element_type=jnp.float32)
        up_product = up_product + adapter_scale * jnp.dot(
            wide_rows, blocks_mat, preferred_element_type=jnp.float32
        )
        summed = lax.psum_scatter(
            jnp.concatenate([gate_term, up_product], axis=1), "tp", scatter_dimension=0, tiled=True
        )
        hidden = (jax.nn.silu(summed[:, :hidden_local]) * summed[:, hidden_local:]).astype(
            jnp.bfloat16
        )
        partial_out = jnp.dot(
            lax.all_gather(hidden, "tp", axis=0, tiled=True),
            down_matrix,
            preferred_element_type=jnp.float32,
        )
        out_total = by_axis(partial_out, POOL)
        outputs.append(out_total.astype(jnp.bfloat16).reshape(group_size, row_count, local_width))
    return jnp.concatenate(outputs, axis=0)


def solution(mesh):
    split = Mesh(mesh.devices.reshape(8, 4, mesh.shape["tp"]), ("pool_0", "pool_1", "tp"))
    return jax.shard_map(
        on_device,
        mesh=split,
        in_specs=(
            P(None, None, "tp"),
            P("tp", POOL),
            P("tp", POOL),
            P(POOL, "tp"),
            P(POOL, None, "tp"),
            P(POOL, "tp", None),
            P(),
            P(),
        ),
        out_specs=P(None, None, "tp"),
        check_vma=False,
    )
```

profile of v0, /device:TPU:8, one launch (start us, length us, event | category | flops | bytes accessed | tf_op | source)
XLA Modules:
  0.0 339.3 jit_solution(7243623281947806800)
XLA Ops:
  6.5 1.1 select_reduce_fusion
  7.7 1.3 fusion.2
  9.6 9.1 %all-to-all-start = ((f32[16,256,4]{1,2,0:T(4,128)}), f32[16,256,4]{1,2,0:T(4,128)S(1)}, u32[]{:S(2)}, u32[]{:S(2)}) async-start(f32[16,256,4]{1,2,0:T(4,128)} %bitcast.7), calls=%async_computation | async-start | bytes 131072 | tf_op jit(solution)/shard_map/all_to_all | solution.py:20
  23.0 3.2 fusion.38
  31.3 2.3 fusion.10
  33.6 1.0 dynamic-slice_select_fusion.1
  35.3 11.7 %all-to-all-start.1 = ((f32[32,256,4]{1,2,0:T(4,128)}), f32[32,256,4]{1,2,0:T(4,128)S(1)}, u32[]{:S(2)}, u32[]{:S(2)}) async-start(f32[32,256,4]{1,2,0:T(4,128)} %broadcast_in_dim.130), calls=%async_computation.1 | async-start | bytes 262144 | tf_op jit(solution)/shard_map/all_to_all | solution.py:26
  47.4 10.3 %all-to-all-done.1 = f32[32,256,4]{1,2,0:T(4,128)S(1)} async-done(((f32[32,256,4]{1,2,0:T(4,128)}), f32[32,256,4]{1,2,0:T(4,128)S(1)}, u32[]{:S(2)}, u32[]{:S(2)}) %all-to-all-start.1) | async-done | bytes 131104 | tf_op jit(solution)/shard_map/all_to_all | solution.py:26
  58.4 3.9 %all-to-all-start.2 = ((bf16[1,4,32,896]{3,1,0,2:T(4,128)(2,1)}), bf16[1,4,32,896]{3,1,0,2:T(4,128)(2,1)S(1)}, u32[]{:S(2)}, u32[]{:S(2)}) async-start(bf16[1,4,32,896]{3,1,0,2:T(4,128)(2,1)} %bitcast.12), calls=%async_computation.2 | async-start | bytes 458752 | tf_op jit(solution)/shard_map/all_to_all | solution.py:96
  62.3 1.0 reduce_sum.108
  64.0 1.5 select_n.160
  65.5 8.2 %all-to-all-done.2 = bf16[1,4,32,896]{3,1,0,2:T(4,128)(2,1)S(1)} async-done(((bf16[1,4,32,896]{3,1,0,2:T(4,128)(2,1)}), bf16[1,4,32,896]{3,1,0,2:T(4,128)(2,1)S(1)}, u32[]{:S(2)}, u32[]{:S(2)}) %all-to-all-start.2) | async-done | bytes 229408 | tf_op jit(solution)/shard_map/all_to_all | solution.py:96
  74.4 1.0 reshape.821
  75.4 1.5 fusion.1
  76.9 1.4 pad_maximum_fusion
  80.1 7.2 %all-to-all-start.3 = ((f32[16,256,4]{1,2,0:T(4,128)}), f32[16,256,4]{1,2,0:T(4,128)S(1)}, u32[]{:S(2)}, u32[]{:S(2)}) async-start(f32[16,256,4]{1,2,0:T(4,128)} %bitcast.23), calls=%async_computation.4 | async-start | bytes 131072 | tf_op jit(solution)/shard_map/all_to_all | solution.py:20
  87.4 1.4 fusion.5
  88.7 5.2 %all-to-all-done.3 = f32[16,256,4]{1,2,0:T(4,128)S(1)} async-done(((f32[16,256,4]{1,2,0:T(4,128)}), f32[16,256,4]{1,2,0:T(4,128)S(1)}, u32[]{:S(2)}, u32[]{:S(2)}) %all-to-all-start.3) | async-done | bytes 65568 | tf_op jit(solution)/shard_map/all_to_all | solution.py:20
  94.6 3.9 %all-to-all-start.4 = ((f32[32,256,4]{1,2,0:T(4,128)}), f32[32,256,4]{1,2,0:T(4,128)S(1)}, u32[]{:S(2)}, u32[]{:S(2)}) async-start(f32[32,256,4]{1,2,0:T(4,128)} %broadcast_in_dim.136), calls=%async_computation.5 | async-start | bytes 262144 | tf_op jit(solution)/shard_map/all_to_all | solution.py:26
  98.9 10.7 %all-to-all-done.4 = f32[32,256,4]{1,2,0:T(4,128)S(1)} async-done(((f32[32,256,4]{1,2,0:T(4,128)}), f32[32,256,4]{1,2,0:T(4,128)S(1)}, u32[]{:S(2)}, u32[]{:S(2)}) %all-to-all-start.4) | async-done | bytes 131104 | tf_op jit(solution)/shard_map/all_to_all | solution.py:26
  109.7 3.9 %all-to-all-start.5 = ((bf16[1,4,32,896]{3,1,0,2:T(4,128)(2,1)}), bf16[1,4,32,896]{3,1,0,2:T(4,128)(2,1)S(1)}, u32[]{:S(2)}, u32[]{:S(2)}) async-start(bf16[1,4,32,896]{3,1,0,2:T(4,128)(2,1)} %bitcast.28), calls=%async_computation.6 | async-start | bytes 458752 | tf_op jit(solution)/shard_map/all_to_all | solution.py:96
  113.7 11.6 %all-to-all-done.5 = bf16[1,4,32,896]{3,1,0,2:T(4,128)(2,1)S(1)} async-done(((bf16[1,4,32,896]{3,1,0,2:T(4,128)(2,1)}), bf16[1,4,32,896]{3,1,0,2:T(4,128)(2,1)S(1)}, u32[]{:S(2)}, u32[]{:S(2)}) %all-to-all-start.5) | async-done | bytes 229408 | tf_op jit(solution)/shard_map/all_to_all | solution.py:96
  125.4 1.5 fusion
  126.9 1.3 pad_maximum_fusion.1
  128.3 4.0 %reduce-scatter.3.cloned.1.call-done = f32[16,1792]{1,0:T(8,128)} async-done(((f32[256,1792]{1,0:T(8,128)}), f32[16,1792]{1,0:T(8,128)}) %reduce-scatter.3.cloned.1.call-update) | async-done | bytes 114704 | tf_op jit(solution)/shard_map/reduce_scatter | solution.py:117
  133.1 18.9 %all_gather.6 = bf16[256,896]{1,0:T(8,128)(2,1)S(1)} all-gather(bf16[16,896]{1,0:T(8,128)(2,1)S(1)} %fusion.23), channel_id=1, replica_groups=mesh['pool_0'=8,'pool_1'=4,'tp'=16] {'tp'}, dimensions={0}, use_global_device_ids=true | all-gather | bytes 487424 | tf_op jit(solution)/shard_map/all_gather | solution.py:124
  152.0 43.8 %reduce-scatter.5.cloned.1.call-done = f32[16,1792]{1,0:T(8,128)} async-done(((f32[256,1792]{1,0:T(8,128)}), f32[16,1792]{1,0:T(8,128)}) %reduce-scatter.5.cloned.1.call-update) | async-done | bytes 114704 | tf_op jit(solution)/shard_map/reduce_scatter | solution.py:117
  196.7 18.9 %all_gather.7 = bf16[256,896]{1,0:T(8,128)(2,1)S(1)} all-gather(bf16[16,896]{1,0:T(8,128)(2,1)S(1)} %fusion.22), channel_id=1, replica_groups=mesh['pool_0'=8,'pool_1'=4,'tp'=16] {'tp'}, dimensions={0}, use_global_device_ids=true | all-gather | bytes 487424 | tf_op jit(solution)/shard_map/all_gather | solution.py:124
  215.6 1.3 fusion.41
  216.8 1.2 fusion.42
  218.1 81.7 %all-reduce.5.cloned.1.call-done = (f32[256,512]{1,0:T(8,128)}, f32[256,512]{1,0:T(8,128)}) async-done(((f32[256,512]{1,0:T(8,128)}, f32[256,512]{1,0:T(8,128)}), (f32[256,512]{1,0:T(8,128)}, f32[256,512]{1,0:T(8,128)})) %all-reduce.5.cloned.1.call-update) | async-done | bytes 1048592 | tf_op jit(solution)/shard_map/psum | solution.py:35
  299.8 32.1 %all-reduce.6 = (bf16[256,512]{1,0:T(8,128)(2,1)S(1)}, bf16[256,512]{1,0:T(8,128)(2,1)S(1)}) all-reduce(f32[256,512]{1,0:T(8,128)} %get-tuple-element.17, f32[256,512]{1,0:T(8,128)} %get-tuple-element.18), channel_id=1, replica_groups=mesh['pool_0'=8,'pool_1'=4,'tp'=16] {'pool_1'}, use_global_device_ids=true, to_apply=%region_20.22 | all-reduce | flops 262144 | bytes 1572864 | tf_op jit(solution)/shard_map/psum | solution.py:35
  (80 shorter events, 15.2 us)
Async XLA Ops:
  6.5 24.7 %copy-start = (bf16[512,896]{1,0:T(8,128)(2,1)S(1)}, bf16[512,896]{1,0:T(8,128)(2,1)}, u32[]{:S(2)}) copy-start(bf16[512,896]{1,0:T(8,128)(2,1)} %param.12) | copy-start | bytes 2752516
  6.5 27.1 %copy-start.6 = (bf16[4,4,28672]{2,1,0:T(4,128)(2,1)S(1)}, bf16[4,4,28672]{2,1,0:T(4,128)(2,1)}, u32[]{:S(2)}) copy-start(bf16[4,4,28672]{2,1,0:T(4,128)(2,1)} %param.15) | copy-start | bytes 2752516
  9.6 25.0 %all-to-all-start = ((f32[16,256,4]{1,2,0:T(4,128)}), f32[16,256,4]{1,2,0:T(4,128)S(1)}, u32[]{:S(2)}, u32[]{:S(2)}) async-start(f32[16,256,4]{1,2,0:T(4,128)} %bitcast.7), calls=%async_computation | async-start | bytes 131072 | tf_op jit(solution)/shard_map/all_to_all | solution.py:20
  27.4 19.6 %copy-start.1 = (bf16[512,896]{1,0:T(8,128)(2,1)S(1)}, bf16[512,896]{1,0:T(8,128)(2,1)}, u32[]{:S(2)}) copy-start(bf16[512,896]{1,0:T(8,128)(2,1)} %param.11) | copy-start | bytes 2752516
  27.4 19.6 %copy-start.3 = (bf16[2,256,512]{2,1,0:T(8,128)(2,1)S(1)}, bf16[2,256,512]{2,1,0:T(8,128)(2,1)}, u32[]{:S(2)}) copy-start(bf16[2,256,512]{2,1,0:T(8,128)(2,1)} %param.10) | copy-start | bytes 1572868
  35.3 22.4 %all-to-all-start.1 = ((f32[32,256,4]{1,2,0:T(4,128)}), f32[32,256,4]{1,2,0:T(4,128)S(1)}, u32[]{:S(2)}, u32[]{:S(2)}) async-start(f32[32,256,4]{1,2,0:T(4,128)} %broadcast_in_dim.130), calls=%async_computation.1 | async-start | bytes 262144 | tf_op jit(solution)/shard_map/all_to_all | solution.py:26
  57.7 0.7 copy-start.5
  58.4 15.3 %all-to-all-start.2 = ((bf16[1,4,32,896]{3,1,0,2:T(4,128)(2,1)}), bf16[1,4,32,896]{3,1,0,2:T(4,128)(2,1)S(1)}, u32[]{:S(2)}, u32[]{:S(2)}) async-start(bf16[1,4,32,896]{3,1,0,2:T(4,128)(2,1)} %bitcast.12), calls=%async_computation.2 | async-start | bytes 458752 | tf_op jit(solution)/shard_map/all_to_all | solution.py:96
  62.3 70.0 %reduce-scatter.3.cloned.1.call-start = ((), (), s32[]{:S(2)}) async-start(), calls=%async_computation.8 | async-start | bytes 1949696 | tf_op jit(solution)/shard_map/reduce_scatter | solution.py:117
  73.7 0.7 copy-start.4
  78.3 0.9 copy-start.7
  80.1 13.8 %all-to-all-start.3 = ((f32[16,256,4]{1,2,0:T(4,128)}), f32[16,256,4]{1,2,0:T(4,128)S(1)}, u32[]{:S(2)}, u32[]{:S(2)}) async-start(f32[16,256,4]{1,2,0:T(4,128)} %bitcast.23), calls=%async_computation.4 | async-start | bytes 131072 | tf_op jit(solution)/shard_map/all_to_all | solution.py:20
  94.6 15.0 %all-to-all-start.4 = ((f32[32,256,4]{1,2,0:T(4,128)}), f32[32,256,4]{1,2,0:T(4,128)S(1)}, u32[]{:S(2)}, u32[]{:S(2)}) async-start(f32[32,256,4]{1,2,0:T(4,128)} %broadcast_in_dim.136), calls=%async_computation.5 | async-start | bytes 262144 | tf_op jit(solution)/shard_map/all_to_all | solution.py:26
  109.7 15.6 %all-to-all-start.5 = ((bf16[1,4,32,896]{3,1,0,2:T(4,128)(2,1)}), bf16[1,4,32,896]{3,1,0,2:T(4,128)(2,1)S(1)}, u32[]{:S(2)}, u32[]{:S(2)}) async-start(bf16[1,4,32,896]{3,1,0,2:T(4,128)(2,1)} %bitcast.28), calls=%async_computation.6 | async-start | bytes 458752 | tf_op jit(solution)/shard_map/all_to_all | solution.py:96
  113.5 82.3 %reduce-scatter.5.cloned.1.call-start = ((), (), s32[]{:S(2)}) async-start(), calls=%async_computation.9 | async-start | bytes 1949696 | tf_op jit(solution)/shard_map/reduce_scatter | solution.py:117
  128.2 87.4 %copy-start.2 = (bf16[896,512]{1,0:T(8,128)(2,1)S(1)}, bf16[896,512]{1,0:T(8,128)(2,1)}, u32[]{:S(2)}) copy-start(bf16[896,512]{1,0:T(8,128)(2,1)} %param.13) | copy-start | bytes 2752516
  128.2 171.6 %all-reduce.5.cloned.1.call-start = ((), (), s32[]{:S(2)}) async-start(), calls=%async_computation.10 | async-start | bytes 2097152 | tf_op jit(solution)/shard_map/psum | solution.py:35
Sparse Core Ops, SparseCore 0:
  78.4 53.7 reduce-scatter.2
  135.1 60.6 reduce-scatter.4
  218.2 81.5 all-reduce.4
where the time goes:
time: 340 us; the launch traced here: 339 us
  waiting for transfers between devices  175 us (51%)
  blocking collectives  70 us (21%)
  starting transfers between devices  39.7 us (12%)
  between operations  17.3 us (5%)
  other arithmetic  14 us (4%)
  matrix products  11.6 us (3%)
  local copies, waits for them, and re-layouts  11.3 us (3%)
    psum x1, waiting for transfers between devices, by_axis(): return functools.reduce(lax.psum, axes, value)  81.7 us
    reduce_scatter x2, waiting for transfers between devices, on_device(): lax.psum_scatter(jnp.concatenate([gate_term, up_product], axis=1), 'tp',...  47.7 us
    all_gather x2, blocking collectives, on_device(): lax.all_gather(hidden, 'tp', axis=0, tiled=True)  37.8 us
    psum x1, blocking collectives, by_axis(): return functools.reduce(lax.psum, axes, value)  32.1 us
    all_to_all x2, waiting for transfers between devices, copy_for_each(): return lax.all_to_all(copies, axis, split_axis=0, concat_axis=0, tiled=True)  21 us
    all_to_all x2, waiting for transfers between devices, on_device(): lax.all_to_all(outgoing, POOL, split_axis=2, concat_axis=0, tiled=True)  19.8 us
    all_to_all x2, starting transfers between devices, sum_at_owner(): pieces = lax.all_to_all(in_blocks(value, dim, size), axis, 0, 0, tiled=True)  16.3 us
    all_to_all x2, starting transfers between devices, copy_for_each(): return lax.all_to_all(copies, axis, split_axis=0, concat_axis=0, tiled=True)  15.5 us
  transfers between devices with their start and end apart: 9, of which 8 were waited for; matrix products, arithmetic and copies ran while one was open for 7% of the time, Pallas kernels for 0%

commit v1 on v0

--- a/solution.py
+++ b/solution.py
@@ -8,6 +8,27 @@
 CAP = 1
 POOL = ("pool_0", "pool_1")
 adapter_scale = 2.0
+
+
+def collect(array, axis, dim):
+    size, mine, span = (lax.axis_size(axis), lax.axis_index(axis), array.shape[dim])
+    right = [(i, (i + 1) % size) for i in range(size)]
+    downward = [(i, (i - 1) % size) for i in range(size)]
+    result = jnp.zeros((*array.shape[:dim], size * span, *array.shape[dim + 1 :]), array.dtype)
+    result = lax.dynamic_update_slice_in_dim(result, array, mine * span, axis=dim)
+    from_left = from_right = array
+    half = size // 2
+    for hop in range(1, half + 1):
+        from_left = lax.ppermute(from_left, axis, right)
+        result = lax.dynamic_update_slice_in_dim(
+            result, from_left, (mine - hop) % size * span, axis=dim
+        )
+        if hop < size - half:
+            from_right = lax.ppermute(from_right, axis, downward)
+            result = lax.dynamic_update_slice_in_dim(
+                result, from_right, (mine + hop) % size * span, axis=dim
+            )
+    return result
 
 
 def in_blocks(value, dim, size):
@@ -121,9 +142,7 @@
             jnp.bfloat16
         )
         partial_out = jnp.dot(
-            lax.all_gather(hidden, "tp", axis=0, tiled=True),
-            down_matrix,
-            preferred_element_type=jnp.float32,
+            collect(hidden, "tp", 0), down_matrix, preferred_element_type=jnp.float32
         )
         out_total = by_axis(partial_out, POOL)
         outputs.append(out_total.astype(jnp.bfloat16).reshape(group_size, row_count, local_width))

time: 340 us -> 368 us (1.082)
  starting transfers between devices: 39.7 us -> 78.1 us
  blocking collectives: 70 us -> 32.1 us
  waiting for transfers between devices: 175 us -> 205 us
    all_gather x2 -> x0, blocking collectives: 37.8 us -> none  [on_device(): lax.all_gather(hidden, 'tp', axis=0, tiled=True)]
    ppermute x0 -> x30, starting transfers between devices: none -> 37.7 us  [the longest x14 37.6 us: collect(): from_right = lax.ppermute(from_right, axis, downward)]
    reduce_scatter x2, waiting for transfers between devices: 47.7 us -> 64.9 us  [on_device(): lax.psum_scatter(jnp.concatenate([gate_term, up_product], axis=1), 'tp',...]
    psum x1, waiting for transfers between devices: 81.7 us -> 87 us  [by_axis(): return functools.reduce(lax.psum, axes, value)]
    ppermute x0 -> x30, waiting for transfers between devices: none -> 4.45 us  [the longest x16 4.41 us: collect(): from_left = lax.ppermute(from_left, axis, right)]
  transfers between devices with their start and end apart: 9 -> 39, of which waited for: 8 -> 10; matrix products, arithmetic and copies ran while one was open for 7% -> 7% of each run, Pallas kernels for 0% -> 0%
where the time goes in v1:
time: 368 us; the launch traced here: 367 us
  waiting for transfers between devices  205 us (56%)
  starting transfers between devices  78.1 us (21%)
  blocking collectives  32.1 us (9%)
  between operations  17.8 us (5%)
  other arithmetic  13.5 us (4%)
  matrix products  11.6 us (3%)
  local copies, waits for them, and re-layouts  9.57 us (3%)
    psum x1, waiting for transfers between devices, by_axis(): return functools.reduce(lax.psum, axes, value)  87 us
    reduce_scatter x2, waiting for transfers between devices, on_device(): lax.psum_scatter(jnp.concatenate([gate_term, up_product], axis=1), 'tp',...  64.9 us
    ppermute x14, starting transfers between devices, collect(): from_right = lax.ppermute(from_right, axis, downward)  37.6 us
    psum x1, blocking collectives, by_axis(): return functools.reduce(lax.psum, axes, value)  32.1 us
    all_to_all x2, waiting for transfers between devices, on_device(): lax.all_to_all(outgoing, POOL, split_axis=2, concat_axis=0, tiled=True)  22.1 us
    all_to_all x2, waiting for transfers between devices, copy_for_each(): return lax.all_to_all(copies, axis, split_axis=0, concat_axis=0, tiled=True)  21 us
    all_to_all x2, starting transfers between devices, sum_at_owner(): pieces = lax.all_to_all(in_blocks(value, dim, size), axis, 0, 0, tiled=True)  16.3 us
    all_to_all x2, starting transfers between devices, copy_for_each(): return lax.all_to_all(copies, axis, split_axis=0, concat_axis=0, tiled=True)  15.5 us
  transfers between devices with their start and end apart: 39, of which 10 were waited for; matrix products, arithmetic and copies ran while one was open for 7% of the time, Pallas kernels for 0%

profile of v1, /device:TPU:8, one launch (start us, length us, event | category | flops | bytes accessed | tf_op | source)
XLA Modules:
  0.0 367.5 jit_solution(8332392556207893232)
XLA Ops:
  9.6 9.1 %all-to-all-start = ((f32[16,256,4]{1,2,0:T(4,128)}), f32[16,256,4]{1,2,0:T(4,128)S(1)}, u32[]{:S(2)}, u32[]{:S(2)}) async-start(f32[16,256,4]{1,2,0:T(4,128)} %bitcast.7), calls=%async_computation | async-start | bytes 131072 | tf_op jit(solution)/shard_map/all_to_all | solution.py:41
  23.0 3.2 fusion.44
  31.2 2.3 fusion.10
  33.5 2.0 dynamic-slice_select_fusion.1
  36.3 11.7 %all-to-all-start.1 = ((f32[32,256,4]{1,2,0:T(4,128)}), f32[32,256,4]{1,2,0:T(4,128)S(1)}, u32[]{:S(2)}, u32[]{:S(2)}) async-start(f32[32,256,4]{1,2,0:T(4,128)} %broadcast_in_dim.130), calls=%async_computation.1 | async-start | bytes 262144 | tf_op jit(solution)/shard_map/all_to_all | solution.py:47
  48.4 10.3 %all-to-all-done.1 = f32[32,256,4]{1,2,0:T(4,128)S(1)} async-done(((f32[32,256,4]{1,2,0:T(4,128)}), f32[32,256,4]{1,2,0:T(4,128)S(1)}, u32[]{:S(2)}, u32[]{:S(2)}) %all-to-all-start.1) | async-done | bytes 131104 | tf_op jit(solution)/shard_map/all_to_all | solution.py:47
  58.7 4.6 %all-to-all-start.2 = ((bf16[1,4,32,896]{3,1,0,2:T(4,128)(2,1)}), bf16[1,4,32,896]{3,1,0,2:T(4,128)(2,1)}, u32[]{:S(2)}, u32[]{:S(2)}) async-start(bf16[1,4,32,896]{3,1,0,2:T(4,128)(2,1)} %bitcast.12), calls=%async_computation.2 | async-start | bytes 458752 | tf_op jit(solution)/shard_map/all_to_all | solution.py:117
  64.1 10.6 %all-to-all-done.2 = bf16[1,4,32,896]{3,1,0,2:T(4,128)(2,1)} async-done(((bf16[1,4,32,896]{3,1,0,2:T(4,128)(2,1)}), bf16[1,4,32,896]{3,1,0,2:T(4,128)(2,1)}, u32[]{:S(2)}, u32[]{:S(2)}) %all-to-all-start.2) | async-done | bytes 229408 | tf_op jit(solution)/shard_map/all_to_all | solution.py:117
  80.5 7.2 %all-to-all-start.3 = ((f32[16,256,4]{1,2,0:T(4,128)}), f32[16,256,4]{1,2,0:T(4,128)S(1)}, u32[]{:S(2)}, u32[]{:S(2)}) async-start(f32[16,256,4]{1,2,0:T(4,128)} %bitcast.23), calls=%async_computation.4 | async-start | bytes 131072 | tf_op jit(solution)/shard_map/all_to_all | solution.py:41
  89.1 5.1 %all-to-all-done.3 = f32[16,256,4]{1,2,0:T(4,128)S(1)} async-done(((f32[16,256,4]{1,2,0:T(4,128)}), f32[16,256,4]{1,2,0:T(4,128)S(1)}, u32[]{:S(2)}, u32[]{:S(2)}) %all-to-all-start.3) | async-done | bytes 65568 | tf_op jit(solution)/shard_map/all_to_all | solution.py:41
  94.9 3.9 %all-to-all-start.4 = ((f32[32,256,4]{1,2,0:T(4,128)}), f32[32,256,4]{1,2,0:T(4,128)S(1)}, u32[]{:S(2)}, u32[]{:S(2)}) async-start(f32[32,256,4]{1,2,0:T(4,128)} %broadcast_in_dim.136), calls=%async_computation.5 | async-start | bytes 262144 | tf_op jit(solution)/shard_map/all_to_all | solution.py:47
  99.2 10.7 %all-to-all-done.4 = f32[32,256,4]{1,2,0:T(4,128)S(1)} async-done(((f32[32,256,4]{1,2,0:T(4,128)}), f32[32,256,4]{1,2,0:T(4,128)S(1)}, u32[]{:S(2)}, u32[]{:S(2)}) %all-to-all-start.4) | async-done | bytes 131104 | tf_op jit(solution)/shard_map/all_to_all | solution.py:47
  110.0 3.9 %all-to-all-start.5 = ((bf16[1,4,32,896]{3,1,0,2:T(4,128)(2,1)}), bf16[1,4,32,896]{3,1,0,2:T(4,128)(2,1)S(1)}, u32[]{:S(2)}, u32[]{:S(2)}) async-start(bf16[1,4,32,896]{3,1,0,2:T(4,128)(2,1)} %bitcast.28), calls=%async_computation.6 | async-start | bytes 458752 | tf_op jit(solution)/shard_map/all_to_all | solution.py:117
  114.1 11.6 %all-to-all-done.5 = bf16[1,4,32,896]{3,1,0,2:T(4,128)(2,1)S(1)} async-done(((bf16[1,4,32,896]{3,1,0,2:T(4,128)(2,1)}), bf16[1,4,32,896]{3,1,0,2:T(4,128)(2,1)S(1)}, u32[]{:S(2)}, u32[]{:S(2)}) %all-to-all-start.5) | async-done | bytes 229408 | tf_op jit(solution)/shard_map/all_to_all | solution.py:117
  128.7 4.0 %reduce-scatter.3.cloned.1.call-done = f32[16,1792]{1,0:T(8,128)} async-done(((f32[256,1792]{1,0:T(8,128)}), f32[16,1792]{1,0:T(8,128)}) %reduce-scatter.3.cloned.1.call-update) | async-done | bytes 114704 | tf_op jit(solution)/shard_map/reduce_scatter | solution.py:138
  133.6 1.7 collective-permute-start.1
  135.3 61.0 %reduce-scatter.5.cloned.1.call-done = f32[16,1792]{1,0:T(8,128)} async-done(((f32[256,1792]{1,0:T(8,128)}), f32[16,1792]{1,0:T(8,128)}) %reduce-scatter.5.cloned.1.call-update) | async-done | bytes 114704 | tf_op jit(solution)/shard_map/reduce_scatter | solution.py:138
  199.0 2.2 collective-permute-start.3
  201.3 2.7 collective-permute-start.18
  204.0 3.0 collective-permute-start.5
  207.0 3.0 collective-permute-start.20
  210.0 2.9 collective-permute-start.7
  213.0 3.0 collective-permute-start.22
  216.0 2.9 collective-permute-start.9
  219.0 3.0 collective-permute-start.24
  222.0 2.9 collective-permute-start.11
  225.0 3.0 collective-permute-start.26
  228.0 2.9 collective-permute-start.13
  231.0 3.0 collective-permute-start.28
  235.5 2.9 collective-permute-done.14
  241.0 87.0 %all-reduce.5.cloned.1.call-done = (f32[256,512]{1,0:T(8,128)}, f32[256,512]{1,0:T(8,128)}) async-done(((f32[256,512]{1,0:T(8,128)}, f32[256,512]{1,0:T(8,128)}), (f32[256,512]{1,0:T(8,128)}, f32[256,512]{1,0:T(8,128)})) %all-reduce.5.cloned.1.call-update) | async-done | bytes 1048592 | tf_op jit(solution)/shard_map/psum | solution.py:56
  327.9 32.1 %all-reduce.6 = (bf16[256,512]{1,0:T(8,128)(2,1)S(1)}, bf16[256,512]{1,0:T(8,128)(2,1)S(1)}) all-reduce(f32[256,512]{1,0:T(8,128)} %get-tuple-element.17, f32[256,512]{1,0:T(8,128)} %get-tuple-element.18), channel_id=1, replica_groups=mesh['pool_0'=8,'pool_1'=4,'tp'=16] {'pool_1'}, use_global_device_ids=true, to_apply=%region_20.22 | all-reduce | flops 262144 | bytes 1572864 | tf_op jit(solution)/shard_map/psum | solution.py:56
  (164 shorter events, 30.4 us)
Async XLA Ops:
  9.6 26.0 %all-to-all-start = ((f32[16,256,4]{1,2,0:T(4,128)}), f32[16,256,4]{1,2,0:T(4,128)S(1)}, u32[]{:S(2)}, u32[]{:S(2)}) async-start(f32[16,256,4]{1,2,0:T(4,128)} %bitcast.7), calls=%async_computation | async-start | bytes 131072 | tf_op jit(solution)/shard_map/all_to_all | solution.py:41
  36.3 22.4 %all-to-all-start.1 = ((f32[32,256,4]{1,2,0:T(4,128)}), f32[32,256,4]{1,2,0:T(4,128)S(1)}, u32[]{:S(2)}, u32[]{:S(2)}) async-start(f32[32,256,4]{1,2,0:T(4,128)} %broadcast_in_dim.130), calls=%async_computation.1 | async-start | bytes 262144 | tf_op jit(solution)/shard_map/all_to_all | solution.py:47
  58.7 16.0 %all-to-all-start.2 = ((bf16[1,4,32,896]{3,1,0,2:T(4,128)(2,1)}), bf16[1,4,32,896]{3,1,0,2:T(4,128)(2,1)}, u32[]{:S(2)}, u32[]{:S(2)}) async-start(bf16[1,4,32,896]{3,1,0,2:T(4,128)(2,1)} %bitcast.12), calls=%async_computation.2 | async-start | bytes 458752 | tf_op jit(solution)/shard_map/all_to_all | solution.py:117
  63.3 69.3 %reduce-scatter.3.cloned.1.call-start = ((), (), s32[]{:S(2)}) async-start(), calls=%async_computation.8 | async-start | bytes 1949696 | tf_op jit(solution)/shard_map/reduce_scatter | solution.py:138
  80.5 13.8 %all-to-all-start.3 = ((f32[16,256,4]{1,2,0:T(4,128)}), f32[16,256,4]{1,2,0:T(4,128)S(1)}, u32[]{:S(2)}, u32[]{:S(2)}) async-start(f32[16,256,4]{1,2,0:T(4,128)} %bitcast.23), calls=%async_computation.4 | async-start | bytes 131072 | tf_op jit(solution)/shard_map/all_to_all | solution.py:41
  94.9 15.1 %all-to-all-start.4 = ((f32[32,256,4]{1,2,0:T(4,128)}), f32[32,256,4]{1,2,0:T(4,128)S(1)}, u32[]{:S(2)}, u32[]{:S(2)}) async-start(f32[32,256,4]{1,2,0:T(4,128)} %broadcast_in_dim.136), calls=%async_computation.5 | async-start | bytes 262144 | tf_op jit(solution)/shard_map/all_to_all | solution.py:47
  110.0 15.7 %all-to-all-start.5 = ((bf16[1,4,32,896]{3,1,0,2:T(4,128)(2,1)}), bf16[1,4,32,896]{3,1,0,2:T(4,128)(2,1)S(1)}, u32[]{:S(2)}, u32[]{:S(2)}) async-start(bf16[1,4,32,896]{3,1,0,2:T(4,128)(2,1)} %bitcast.28), calls=%async_computation.6 | async-start | bytes 458752 | tf_op jit(solution)/shard_map/all_to_all | solution.py:117
  113.9 82.4 %reduce-scatter.5.cloned.1.call-start = ((), (), s32[]{:S(2)}) async-start(), calls=%async_computation.9 | async-start | bytes 1949696 | tf_op jit(solution)/shard_map/reduce_scatter | solution.py:138
  128.6 199.3 %all-reduce.5.cloned.1.call-start = ((), (), s32[]{:S(2)}) async-start(), calls=%async_computation.10 | async-start | bytes 2097152 | tf_op jit(solution)/shard_map/psum | solution.py:56
  133.5 65.4 %collective-permute-start = (bf16[16,896]{1,0:T(8,128)(2,1)S(1)}, bf16[16,896]{1,0:T(8,128)(2,1)S(1)}, u32[]{:S(2)}, u32[]{:S(2)}) collective-permute-start(bf16[16,896]{1,0:T(8,128)(2,1)S(1)} %get-tuple-element.22), channel_id=1, source_target_pairs={{0,1},{1,2},{2,3},{3,4},{4,5},{5,6},{6,7},{7,8},{8,9},{9,10},{10,1... | collective-permute-start | bytes 86024 | tf_op jit(solution)/shard_map/ppermute | solution.py:22
  133.6 65.4 %collective-permute-start.1 = (bf16[16,896]{1,0:T(8,128)(2,1)S(1)}, bf16[16,896]{1,0:T(8,128)(2,1)S(1)}, u32[]{:S(2)}, u32[]{:S(2)}) collective-permute-start(bf16[16,896]{1,0:T(8,128)(2,1)S(1)} %get-tuple-element.22), channel_id=1, source_target_pairs={{0,15},{1,0},{2,1},{3,2},{4,3},{5,4},{6,5},{7,6},{8,7},{9,8},{10,9... | collective-permute-start | bytes 86024 | tf_op jit(solution)/shard_map/ppermute | solution.py:27
  199.0 5.0 %collective-permute-start.3 = (bf16[16,896]{1,0:T(8,128)(2,1)S(1)}, bf16[16,896]{1,0:T(8,128)(2,1)S(1)}, u32[]{:S(2)}, u32[]{:S(2)}) collective-permute-start(bf16[16,896]{1,0:T(8,128)(2,1)S(1)} %collective-permute-done.1), channel_id=1, source_target_pairs={{0,15},{1,0},{2,1},{3,2},{4,3},{5,4},{6,5},{7,6},{8,7},{9,8},{10,9... | collective-permute-start | bytes 86024 | tf_op jit(solution)/shard_map/ppermute | solution.py:27
  201.2 5.7 %collective-permute-start.17 = (bf16[16,896]{1,0:T(8,128)(2,1)S(1)}, bf16[16,896]{1,0:T(8,128)(2,1)S(1)}, u32[]{:S(2)}, u32[]{:S(2)}) collective-permute-start(bf16[16,896]{1,0:T(8,128)(2,1)S(1)} %collective-permute-done.15), channel_id=1, source_target_pairs={{0,1},{1,2},{2,3},{3,4},{4,5},{5,6},{6,7},{7,8},{8,9},{9,10},{10,1... | collective-permute-start | bytes 86024 | tf_op jit(solution)/shard_map/ppermute | solution.py:22
  201.3 5.7 %collective-permute-start.18 = (bf16[16,896]{1,0:T(8,128)(2,1)S(1)}, bf16[16,896]{1,0:T(8,128)(2,1)S(1)}, u32[]{:S(2)}, u32[]{:S(2)}) collective-permute-start(bf16[16,896]{1,0:T(8,128)(2,1)S(1)} %collective-permute-done.16), channel_id=1, source_target_pairs={{0,15},{1,0},{2,1},{3,2},{4,3},{5,4},{6,5},{7,6},{8,7},{9,8},{10,9... | collective-permute-start | bytes 86024 | tf_op jit(solution)/shard_map/ppermute | solution.py:27
  204.0 6.0 %collective-permute-start.4 = (bf16[16,896]{1,0:T(8,128)(2,1)S(1)}, bf16[16,896]{1,0:T(8,128)(2,1)S(1)}, u32[]{:S(2)}, u32[]{:S(2)}) collective-permute-start(bf16[16,896]{1,0:T(8,128)(2,1)S(1)} %collective-permute-done.2), channel_id=1, source_target_pairs={{0,1},{1,2},{2,3},{3,4},{4,5},{5,6},{6,7},{7,8},{8,9},{9,10},{10,1... | collective-permute-start | bytes 86024 | tf_op jit(solution)/shard_map/ppermute | solution.py:22
  204.0 6.0 %collective-permute-start.5 = (bf16[16,896]{1,0:T(8,128)(2,1)S(1)}, bf16[16,896]{1,0:T(8,128)(2,1)S(1)}, u32[]{:S(2)}, u32[]{:S(2)}) collective-permute-start(bf16[16,896]{1,0:T(8,128)(2,1)S(1)} %collective-permute-done.3), channel_id=1, source_target_pairs={{0,15},{1,0},{2,1},{3,2},{4,3},{5,4},{6,5},{7,6},{8,7},{9,8},{10,9... | collective-permute-start | bytes 86024 | tf_op jit(solution)/shard_map/ppermute | solution.py:27
  207.0 6.0 %collective-permute-start.19 = (bf16[16,896]{1,0:T(8,128)(2,1)S(1)}, bf16[16,896]{1,0:T(8,128)(2,1)S(1)}, u32[]{:S(2)}, u32[]{:S(2)}) collective-permute-start(bf16[16,896]{1,0:T(8,128)(2,1)S(1)} %collective-permute-done.17), channel_id=1, source_target_pairs={{0,1},{1,2},{2,3},{3,4},{4,5},{5,6},{6,7},{7,8},{8,9},{9,10},{10,1... | collective-permute-start | bytes 86024 | tf_op jit(solution)/shard_map/ppermute | solution.py:22
  207.0 6.0 %collective-permute-start.20 = (bf16[16,896]{1,0:T(8,128)(2,1)S(1)}, bf16[16,896]{1,0:T(8,128)(2,1)S(1)}, u32[]{:S(2)}, u32[]{:S(2)}) collective-permute-start(bf16[16,896]{1,0:T(8,128)(2,1)S(1)} %collective-permute-done.18), channel_id=1, source_target_pairs={{0,15},{1,0},{2,1},{3,2},{4,3},{5,4},{6,5},{7,6},{8,7},{9,8},{10,9... | collective-permute-start | bytes 86024 | tf_op jit(solution)/shard_map/ppermute | solution.py:27
  210.0 6.0 %collective-permute-start.6 = (bf16[16,896]{1,0:T(8,128)(2,1)S(1)}, bf16[16,896]{1,0:T(8,128)(2,1)S(1)}, u32[]{:S(2)}, u32[]{:S(2)}) collective-permute-start(bf16[16,896]{1,0:T(8,128)(2,1)S(1)} %collective-permute-done.4), channel_id=1, source_target_pairs={{0,1},{1,2},{2,3},{3,4},{4,5},{5,6},{6,7},{7,8},{8,9},{9,10},{10,1... | collective-permute-start | bytes 86024 | tf_op jit(solution)/shard_map/ppermute | solution.py:22
  210.0 6.0 %collective-permute-start.7 = (bf16[16,896]{1,0:T(8,128)(2,1)S(1)}, bf16[16,896]{1,0:T(8,128)(2,1)S(1)}, u32[]{:S(2)}, u32[]{:S(2)}) collective-permute-start(bf16[16,896]{1,0:T(8,128)(2,1)S(1)} %collective-permute-done.5), channel_id=1, source_target_pairs={{0,15},{1,0},{2,1},{3,2},{4,3},{5,4},{6,5},{7,6},{8,7},{9,8},{10,9... | collective-permute-start | bytes 86024 | tf_op jit(solution)/shard_map/ppermute | solution.py:27
  212.9 6.0 %collective-permute-start.21 = (bf16[16,896]{1,0:T(8,128)(2,1)S(1)}, bf16[16,896]{1,0:T(8,128)(2,1)S(1)}, u32[]{:S(2)}, u32[]{:S(2)}) collective-permute-start(bf16[16,896]{1,0:T(8,128)(2,1)S(1)} %collective-permute-done.19), channel_id=1, source_target_pairs={{0,1},{1,2},{2,3},{3,4},{4,5},{5,6},{6,7},{7,8},{8,9},{9,10},{10,1... | collective-permute-start | bytes 86024 | tf_op jit(solution)/shard_map/ppermute | solution.py:22
  213.0 6.0 %collective-permute-start.22 = (bf16[16,896]{1,0:T(8,128)(2,1)S(1)}, bf16[16,896]{1,0:T(8,128)(2,1)S(1)}, u32[]{:S(2)}, u32[]{:S(2)}) collective-permute-start(bf16[16,896]{1,0:T(8,128)(2,1)S(1)} %collective-permute-done.20), channel_id=1, source_target_pairs={{0,15},{1,0},{2,1},{3,2},{4,3},{5,4},{6,5},{7,6},{8,7},{9,8},{10,9... | collective-permute-start | bytes 86024 | tf_op jit(solution)/shard_map/ppermute | solution.py:27
  216.0 6.0 %collective-permute-start.8 = (bf16[16,896]{1,0:T(8,128)(2,1)S(1)}, bf16[16,896]{1,0:T(8,128)(2,1)S(1)}, u32[]{:S(2)}, u32[]{:S(2)}) collective-permute-start(bf16[16,896]{1,0:T(8,128)(2,1)S(1)} %collective-permute-done.6), channel_id=1, source_target_pairs={{0,1},{1,2},{2,3},{3,4},{4,5},{5,6},{6,7},{7,8},{8,9},{9,10},{10,1... | collective-permute-start | bytes 86024 | tf_op jit(solution)/shard_map/ppermute | solution.py:22
  216.0 6.0 %collective-permute-start.9 = (bf16[16,896]{1,0:T(8,128)(2,1)S(1)}, bf16[16,896]{1,0:T(8,128)(2,1)S(1)}, u32[]{:S(2)}, u32[]{:S(2)}) collective-permute-start(bf16[16,896]{1,0:T(8,128)(2,1)S(1)} %collective-permute-done.7), channel_id=1, source_target_pairs={{0,15},{1,0},{2,1},{3,2},{4,3},{5,4},{6,5},{7,6},{8,7},{9,8},{10,9... | collective-permute-start | bytes 86024 | tf_op jit(solution)/shard_map/ppermute | solution.py:27
  218.9 6.0 %collective-permute-start.23 = (bf16[16,896]{1,0:T(8,128)(2,1)S(1)}, bf16[16,896]{1,0:T(8,128)(2,1)S(1)}, u32[]{:S(2)}, u32[]{:S(2)}) collective-permute-start(bf16[16,896]{1,0:T(8,128)(2,1)S(1)} %collective-permute-done.21), channel_id=1, source_target_pairs={{0,1},{1,2},{2,3},{3,4},{4,5},{5,6},{6,7},{7,8},{8,9},{9,10},{10,1... | collective-permute-start | bytes 86024 | tf_op jit(solution)/shard_map/ppermute | solution.py:22
  219.0 6.0 %collective-permute-start.24 = (bf16[16,896]{1,0:T(8,128)(2,1)S(1)}, bf16[16,896]{1,0:T(8,128)(2,1)S(1)}, u32[]{:S(2)}, u32[]{:S(2)}) collective-permute-start(bf16[16,896]{1,0:T(8,128)(2,1)S(1)} %collective-permute-done.22), channel_id=1, source_target_pairs={{0,15},{1,0},{2,1},{3,2},{4,3},{5,4},{6,5},{7,6},{8,7},{9,8},{10,9... | collective-permute-start | bytes 86024 | tf_op jit(solution)/shard_map/ppermute | solution.py:27
  222.0 6.0 %collective-permute-start.10 = (bf16[16,896]{1,0:T(8,128)(2,1)S(1)}, bf16[16,896]{1,0:T(8,128)(2,1)S(1)}, u32[]{:S(2)}, u32[]{:S(2)}) collective-permute-start(bf16[16,896]{1,0:T(8,128)(2,1)S(1)} %collective-permute-done.8), channel_id=1, source_target_pairs={{0,1},{1,2},{2,3},{3,4},{4,5},{5,6},{6,7},{7,8},{8,9},{9,10},{10,1... | collective-permute-start | bytes 86024 | tf_op jit(solution)/shard_map/ppermute | solution.py:22
  222.0 6.0 %collective-permute-start.11 = (bf16[16,896]{1,0:T(8,128)(2,1)S(1)}, bf16[16,896]{1,0:T(8,128)(2,1)S(1)}, u32[]{:S(2)}, u32[]{:S(2)}) collective-permute-start(bf16[16,896]{1,0:T(8,128)(2,1)S(1)} %collective-permute-done.9), channel_id=1, source_target_pairs={{0,15},{1,0},{2,1},{3,2},{4,3},{5,4},{6,5},{7,6},{8,7},{9,8},{10,9... | collective-permute-start | bytes 86024 | tf_op jit(solution)/shard_map/ppermute | solution.py:27
  224.9 6.0 %collective-permute-start.25 = (bf16[16,896]{1,0:T(8,128)(2,1)S(1)}, bf16[16,896]{1,0:T(8,128)(2,1)S(1)}, u32[]{:S(2)}, u32[]{:S(2)}) collective-permute-start(bf16[16,896]{1,0:T(8,128)(2,1)S(1)} %collective-permute-done.23), channel_id=1, source_target_pairs={{0,1},{1,2},{2,3},{3,4},{4,5},{5,6},{6,7},{7,8},{8,9},{9,10},{10,1... | collective-permute-start | bytes 86024 | tf_op jit(solution)/shard_map/ppermute | solution.py:22
  225.0 6.0 %collective-permute-start.26 = (bf16[16,896]{1,0:T(8,128)(2,1)S(1)}, bf16[16,896]{1,0:T(8,128)(2,1)S(1)}, u32[]{:S(2)}, u32[]{:S(2)}) collective-permute-start(bf16[16,896]{1,0:T(8,128)(2,1)S(1)} %collective-permute-done.24), channel_id=1, source_target_pairs={{0,15},{1,0},{2,1},{3,2},{4,3},{5,4},{6,5},{7,6},{8,7},{9,8},{10,9... | collective-permute-start | bytes 86024 | tf_op jit(solution)/shard_map/ppermute | solution.py:27
  228.0 6.0 %collective-permute-start.12 = (bf16[16,896]{1,0:T(8,128)(2,1)S(1)}, bf16[16,896]{1,0:T(8,128)(2,1)S(1)}, u32[]{:S(2)}, u32[]{:S(2)}) collective-permute-start(bf16[16,896]{1,0:T(8,128)(2,1)S(1)} %collective-permute-done.10), channel_id=1, source_target_pairs={{0,1},{1,2},{2,3},{3,4},{4,5},{5,6},{6,7},{7,8},{8,9},{9,10},{10,1... | collective-permute-start | bytes 86024 | tf_op jit(solution)/shard_map/ppermute | solution.py:22
  228.0 7.5 %collective-permute-start.13 = (bf16[16,896]{1,0:T(8,128)(2,1)S(1)}, bf16[16,896]{1,0:T(8,128)(2,1)S(1)}, u32[]{:S(2)}, u32[]{:S(2)}) collective-permute-start(bf16[16,896]{1,0:T(8,128)(2,1)S(1)} %collective-permute-done.11), channel_id=1, source_target_pairs={{0,15},{1,0},{2,1},{3,2},{4,3},{5,4},{6,5},{7,6},{8,7},{9,8},{10,9... | collective-permute-start | bytes 86024 | tf_op jit(solution)/shard_map/ppermute | solution.py:27
  (12 other events, 207.3 us)
Sparse Core Ops, SparseCore 0:
  78.8 53.8 reduce-scatter.2
  135.4 60.7 reduce-scatter.4
  241.1 86.7 all-reduce.4
